TPU v7x, 256 devices: a whole 4x4x8 slice. The times are simulated.
256 devices in a mesh: lon: 128 (over x, z, y), lat: 2 (over core).
Axes of the slice: x: 4, y: 4, z: 8, core: 2. Of those that a mesh axis runs over, the one named last changes fastest.
Arguments:
- ensemble: float32 [64, 2048, 2048], P(None, 'lon', 'lat'), may hold values from -6 to 6
- obs_lon: int32 [6, 16], replicated, may hold values from 0 to 15
- obs_lat: int32 [6, 16], replicated, may hold values from 0 to 1023
- obs_offset: float32 [6, 2, 16], replicated, may hold values from -0.5 to 0.5
- obs_value: float32 [6, 16], replicated, may hold values from -6 to 6
- obs_error: float32 [6, 16], replicated, may hold values from 0.2 to 2
- owners: int32 [6], replicated, may hold values from 0 to 255
- group_order: int32 [6], replicated, may hold values from 0 to 5, each once
Outputs:
- analysis: float32 [64, 2048, 2048], P(None, 'lon', 'lat')
Inputs may be any that keep to these rules, and one draw needn't show every extreme that they name: `owners`: a tile number: longitude tile index times 2 plus latitude tile index. `group_order`: each group once.
All inputs are finite; a program needn't handle non-finite values.
Results may differ from a plain program's by a relative error of at most 0.00024.
Values sent between devices are 32-bit elements; how exact they have to be, the bound alone decides.
No kernel may reach another device: no remote copies, remote signals or barrier semaphores. Data moves between devices by JAX's collectives and lax.ppermute only.
A program may use at most 64 MiB of HBM per device.

v0:
```python
import jax
import jax.numpy as jnp
from jax import lax
from jax.sharding import Mesh
from jax.sharding import PartitionSpec as P

LON = ("lon_0", "lon_1", "lon_2")
LON_LAT = ("lon_0", "lon_1", "lon_2", "lat")


precise = lax.Precision.HIGHEST


def one_axis_at_a_time(shard, axes):
    for axis in axes:
        shard = lax.psum(shard, axis)
    return shard


def hat_weights(offset):
    return jnp.stack([jnp.maximum(-offset, 0.0), 1.0 - jnp.abs(offset), jnp.maximum(offset, 0.0)])


def serial_update(prior_rows, values, errors):
    members = prior_rows.shape[1]
    scale = jnp.float32(members - 1)

    def one_step(obs_index, carried):
        current_rows, transform = carried
        current = lax.dynamic_index_in_dim(current_rows, obs_index, 0, keepdims=False)
        value = lax.dynamic_index_in_dim(values, obs_index, 0, keepdims=False)
        error = lax.dynamic_index_in_dim(errors, obs_index, 0, keepdims=False)
        mean_row = jnp.mean(current)
        spread = current - mean_row
        variance = jnp.sum(spread * spread) / scale + error
        shrink = 1.0 / (1.0 + jnp.sqrt(error / variance))
        direction = (value - mean_row - shrink * spread) / (scale * variance)
        current_rows = current_rows + jnp.outer(
            jnp.dot(current_rows, spread, precision=precise), direction
        )
        transform = transform + jnp.outer(jnp.dot(transform, spread, precision=precise), direction)
        return (current_rows, transform)

    start = (prior_rows, jnp.eye(members, dtype=jnp.float32))
    return lax.fori_loop(0, prior_rows.shape[0], one_step, start)[1]


def apply_transform(field, transform):
    flattened = field.reshape(field.shape[0], -1)
    return jnp.dot(transform.T, flattened, precision=precise).reshape(field.shape)


def body(ensemble, obs_lon, obs_lat, obs_offset, obs_value, obs_error, owners, group_order):
    members, lon_cells_dev, lat_cells_dev = ensemble.shape
    lat_tiles = lax.axis_size("lat")
    my_lon = lax.axis_index(LON)
    my_lat = lax.axis_index("lat")
    groups = group_order.shape[0]
    obs_count = obs_lon.shape[1]
    total = jnp.eye(members, dtype=jnp.float32)
    for position in range(groups):
        group_id = group_order[position]
        offsets = obs_offset[group_id]
        lon_hat = hat_weights(offsets[0])
        lat_hat = hat_weights(offsets[1])
        stencil_sum = jnp.zeros((members, obs_count), jnp.float32)
        owner_tile = owners[group_id]
        lon_cells = (owner_tile // lat_tiles - my_lon) * lon_cells_dev + obs_lon[group_id]
        lat_cells = (owner_tile % lat_tiles - my_lat) * lat_cells_dev + obs_lat[group_id]
        for lon_step in range(3):
            for lat_step in range(3):
                lon_idx = lon_cells + (lon_step - 1)
                lat_idx = lat_cells + (lat_step - 1)
                inside = (
                    (lon_idx >= 0)
                    & (lon_idx < lon_cells_dev)
                    & (lat_idx >= 0)
                    & (lat_idx < lat_cells_dev)
                ).astype(jnp.float32)
                picked = ensemble[
                    :,
                    jnp.clip(lon_idx, 0, lon_cells_dev - 1),
                    jnp.clip(lat_idx, 0, lat_cells_dev - 1),
                ]
                stencil_sum = (
                    stencil_sum + picked * (lon_hat[lon_step] * lat_hat[lat_step] * inside)[None, :]
                )
        first_rows = one_axis_at_a_time(stencil_sum, LON_LAT)
        prior_rows = jnp.dot(first_rows.T, total, precision=precise)
        group_step = serial_update(prior_rows, obs_value[group_id], obs_error[group_id])
        total = jnp.dot(total, group_step, precision=precise)
    return apply_transform(ensemble, total)


def solution(mesh):
    torus = Mesh(
        mesh.devices.reshape(4, 8, 4, mesh.shape["lat"]), ("lon_0", "lon_1", "lon_2", "lat")
    )
    in_specs = (P(None, LON, "lat"), P(), P(), P(), P(), P(), P(), P())
    out_specs = P(None, LON, "lat")
    return jax.shard_map(body, mesh=torus, in_specs=in_specs, out_specs=out_specs, check_vma=False)
```

profile of v0, /device:TPU:1, one launch (start us, length us, event | category | flops | bytes accessed | tf_op | source)
XLA Modules:
  0.0 752.7 jit_solution(10985909592167883337)
XLA Ops:
  0.0 7.1 copy.64
  27.6 1.8 gather_fusion.8
  33.0 1.8 gather_fusion.5
  34.8 1.8 gather_fusion.4
  36.6 1.8 gather_fusion.3
  38.5 1.8 gather_fusion.2
  40.3 1.8 gather_fusion.1
  42.1 1.8 gather_fusion
  44.1 1.8 gather_fusion.17
  45.9 1.8 gather_fusion.16
  92.3 1.8 gather_fusion.44
  108.8 1.8 gather_fusion.53
  125.2 15.9 %all-reduce.2 = (f32[64,16]{0,1:T(8,128)S(1)}, f32[64,16]{0,1:T(8,128)S(1)}, f32[64,16]{0,1:T(8,128)S(1)}, f32[64,16]{0,1:T(8,128)S(1)}, f32[64,16]{0,1:T(8,128)S(1)}, /*index=5*/f32[64,16]{0,1:T(8,128)S(1)}) all-reduce(f32[64,16]{0,1:T(8,128)S(1)} %bitcast_add_fusion.5, ...), channel_id=1, replica_groups=mesh['lon_0'=4,'lon_1'=8,'lon_2'=4,'lat'=2] {'lon_0'}, use_global_device_ids=true, to_apply=%region_0.1 | all-reduce | flops 6144 | bytes 49152 | tf_op jit(solution)/shard_map/psum | solution.py:16
  141.1 26.0 %all-reduce = (f32[64,16]{0,1:T(8,128)S(1)}, f32[64,16]{0,1:T(8,128)S(1)}, f32[64,16]{0,1:T(8,128)S(1)}, f32[64,16]{0,1:T(8,128)S(1)}, f32[64,16]{0,1:T(8,128)S(1)}, /*index=5*/f32[64,16]{0,1:T(8,128)S(1)}) all-reduce(f32[64,16]{0,1:T(8,128)S(1)} %get-tuple-element.647, ...), channel_id=1, replica_groups=mesh['lon_0'=4,'lon_1'=8,'lon_2'=4,'lat'=2] {'lon_1'}, use_global_device_ids=true, to_apply=%region_1.2 | all-reduce | flops 6144 | bytes 49152 | tf_op jit(solution)/shard_map/psum | solution.py:16
  167.1 14.1 %all-reduce.1 = (f32[64,16]{0,1:T(8,128)S(1)}, f32[64,16]{0,1:T(8,128)S(1)}, f32[64,16]{0,1:T(8,128)S(1)}, f32[64,16]{0,1:T(8,128)S(1)}, f32[64,16]{0,1:T(8,128)S(1)}, /*index=5*/f32[64,16]{0,1:T(8,128)S(1)}) all-reduce(f32[64,16]{0,1:T(8,128)S(1)} %get-tuple-element.635, ...), channel_id=1, replica_groups=mesh['lon_0'=4,'lon_1'=8,'lon_2'=4,'lat'=2] {'lon_2'}, use_global_device_ids=true, to_apply=%region_2.3 | all-reduce | flops 6144 | bytes 49152 | tf_op jit(solution)/shard_map/psum | solution.py:16
  181.2 3.7 all-reduce.3
  185.1 92.1 %while.90 = (s32[]{:T(128)}, f32[16,64]{1,0:T(8,128)S(1)}, f32[64,64]{1,0:T(8,128)S(1)}, f32[16]{0:T(128)S(1)}, f32[16]{0:T(128)S(1)}, /*index=5*/s32[]{:T(128)}, f32[]{:T(128)}, f32[]{:T(128)}, f32[]{:T(128)}, f32[]{:T(128)}) while((s32[]{:T(128)}, f32[16,64]{1,0:T(8,128)S(1)}, f32[64,64]{1,0:T(8,128)S(1)}, f32[16]{0:T(128)S(1)}, ...), condition=%wide.region_7.8_spmd, body=%wide.region_4.7_spmd.sunk | while | flops 72136 | bytes 64653 | solution.py:45
  277.6 92.1 %while.91 = (s32[]{:T(128)}, f32[16,64]{1,0:T(8,128)S(1)}, f32[64,64]{1,0:T(8,128)S(1)}, f32[16]{0:T(128)S(1)}, f32[16]{0:T(128)S(1)}, /*index=5*/s32[]{:T(128)}, f32[]{:T(128)}, f32[]{:T(128)}, f32[]{:T(128)}, f32[]{:T(128)}) while((s32[]{:T(128)}, f32[16,64]{1,0:T(8,128)S(1)}, f32[64,64]{1,0:T(8,128)S(1)}, f32[16]{0:T(128)S(1)}, ...), condition=%wide.region_15.16_spmd, body=%wide.region_12.15_spmd.sunk | while | flops 72136 | bytes 64653 | solution.py:45
  370.1 92.1 %while.92 = (s32[]{:T(128)}, f32[16,64]{1,0:T(8,128)S(1)}, f32[64,64]{1,0:T(8,128)S(1)}, f32[16]{0:T(128)S(1)}, f32[16]{0:T(128)S(1)}, /*index=5*/s32[]{:T(128)}, f32[]{:T(128)}, f32[]{:T(128)}, f32[]{:T(128)}, f32[]{:T(128)}) while((s32[]{:T(128)}, f32[16,64]{1,0:T(8,128)S(1)}, f32[64,64]{1,0:T(8,128)S(1)}, f32[16]{0:T(128)S(1)}, ...), condition=%wide.region_23.24_spmd, body=%wide.region_20.23_spmd.sunk | while | flops 72136 | bytes 64653 | solution.py:45
  462.6 92.1 %while.93 = (s32[]{:T(128)}, f32[16,64]{1,0:T(8,128)S(1)}, f32[64,64]{1,0:T(8,128)S(1)}, f32[16]{0:T(128)S(1)}, f32[16]{0:T(128)S(1)}, /*index=5*/s32[]{:T(128)}, f32[]{:T(128)}, f32[]{:T(128)}, f32[]{:T(128)}, f32[]{:T(128)}) while((s32[]{:T(128)}, f32[16,64]{1,0:T(8,128)S(1)}, f32[64,64]{1,0:T(8,128)S(1)}, f32[16]{0:T(128)S(1)}, ...), condition=%wide.region_31.32_spmd, body=%wide.region_28.31_spmd.sunk | while | flops 72136 | bytes 64653 | solution.py:45
  555.1 92.1 %while.94 = (s32[]{:T(128)}, f32[16,64]{1,0:T(8,128)S(1)}, f32[64,64]{1,0:T(8,128)S(1)}, f32[16]{0:T(128)S(1)}, f32[16]{0:T(128)S(1)}, /*index=5*/s32[]{:T(128)}, f32[]{:T(128)}, f32[]{:T(128)}, f32[]{:T(128)}, f32[]{:T(128)}) while((s32[]{:T(128)}, f32[16,64]{1,0:T(8,128)S(1)}, f32[64,64]{1,0:T(8,128)S(1)}, f32[16]{0:T(128)S(1)}, ...), condition=%wide.region_39.40_spmd, body=%wide.region_36.39_spmd.sunk | while | flops 72136 | bytes 64653 | solution.py:45
  647.6 92.1 %while.95 = (s32[]{:T(128)}, f32[16,64]{1,0:T(8,128)S(1)}, f32[64,64]{1,0:T(8,128)S(1)}, f32[16]{0:T(128)S(1)}, f32[16]{0:T(128)S(1)}, /*index=5*/s32[]{:T(128)}, f32[]{:T(128)}, f32[]{:T(128)}, f32[]{:T(128)}, f32[]{:T(128)}) while((s32[]{:T(128)}, f32[16,64]{1,0:T(8,128)S(1)}, f32[64,64]{1,0:T(8,128)S(1)}, f32[16]{0:T(128)S(1)}, ...), condition=%wide.region_47.48_spmd, body=%wide.region_44.47_spmd.sunk | while | flops 72136 | bytes 64653 | solution.py:45
  740.0 8.2 %fusion.24 = f32[64,16,1024]{2,0,1:T(8,128)S(1)} fusion(f32[64,64,1]{0,1,2:T(8,128)S(1)} %convolution_bitcast_fusion.12, f32[8,8,16,1024]{3,2,1,0:T(8,128)} %bitcast.876), kind=kOutput, calls=%fused_computation.126 | convolution fusion | flops 805306368 | bytes 8404992 | tf_op jit(solution)/shard_map/dot_general | solution.py:50
  748.2 4.4 copy.119
  (975 shorter events, 345.9 us)
Async XLA Ops:
  0.0 19.2 %copy-start.2 = (f32[6,2,16]{2,1,0:T(2,128)S(1)}, f32[6,2,16]{2,1,0:T(2,128)}, u32[]{:S(2)}) copy-start(f32[6,2,16]{2,1,0:T(2,128)} %param.23) | copy-start | bytes 2308
  0.0 7.1 copy-start
  0.0 27.5 %copy-start.5 = (s32[6,16]{1,0:T(8,128)S(1)}, s32[6,16]{1,0:T(8,128)}, u32[]{:S(2)}) copy-start(s32[6,16]{1,0:T(8,128)} %param.22) | copy-start | bytes 1156
  0.0 19.2 %copy-start.1 = (s32[6]{0:T(128)S(1)}, s32[6]{0:T(128)}, u32[]{:S(2)}) copy-start(s32[6]{0:T(128)} %param.26) | copy-start | bytes 76
  0.0 27.5 %copy-start.6 = (s32[6,16]{1,0:T(8,128)S(1)}, s32[6,16]{1,0:T(8,128)}, u32[]{:S(2)}) copy-start(s32[6,16]{1,0:T(8,128)} %param.21) | copy-start | bytes 1156
  33.0 152.1 %copy-start.3 = (f32[6,16]{1,0:T(8,128)S(1)}, f32[6,16]{1,0:T(8,128)}, u32[]{:S(2)}) copy-start(f32[6,16]{1,0:T(8,128)} %param.24) | copy-start | bytes 1156
  33.0 152.1 %copy-start.4 = (f32[6,16]{1,0:T(8,128)S(1)}, f32[6,16]{1,0:T(8,128)}, u32[]{:S(2)}) copy-start(f32[6,16]{1,0:T(8,128)} %param.25) | copy-start | bytes 1156
where the time goes:
time: 764 us; the launch traced here: 753 us
  loops' own time  280 us (37%)
  local copies, waits for them, and re-layouts  213 us (28%)
  other arithmetic  135 us (18%)
  blocking collectives  59.7 us (8%)
  matrix products  36.9 us (5%)
  between operations  27.3 us (4%)
    another operation x6, loops' own time, serial_update(): return lax.fori_loop(0, prior_rows.shape[0], one_step, start)[1]  280 us
    gather x54, local copies, waits for them, and re-layouts, body(): ensemble[:, jnp.clip(lon_idx, 0, lon_cells_dev - 1), jnp.clip(lat_idx, 0,...  88.7 us
    reduce_sum x96, other arithmetic, one_step(): mean_row = jnp.mean(current)  60.7 us
    psum x4, blocking collectives, one_axis_at_a_time(): shard = lax.psum(shard, axis)  59.7 us
    reduce_sum x96, other arithmetic, one_step(): variance = jnp.sum(spread * spread) / scale + error  58 us
    dynamic_slice x96, local copies, waits for them, and re-layouts, one_step(): value = lax.dynamic_index_in_dim(values, obs_index, 0, keepdims=False)  55.9 us
    dynamic_slice x96, local copies, waits for them, and re-layouts, one_step(): error = lax.dynamic_index_in_dim(errors, obs_index, 0, keepdims=False)  55.9 us

commit v1 on v0

v1 whole, which is shorter than its diff:
```python
import functools

import jax
import jax.numpy as jnp
from jax import lax
from jax.experimental import pallas as pl
from jax.experimental.pallas import tpu as pltpu
from jax.sharding import Mesh
from jax.sharding import PartitionSpec as P

LON = ("lon_0", "lon_1", "lon_2")
LANES = 128
HIGH = lax.Precision.HIGHEST


def priors_kernel(
    sizes, place, lon_in, lat_in, offset_in, value_in, error_in, owners_in, order_in, field,
    rows_t, table, lon, lat, offset, value, error, owners, order, tile, small_sems, sems
):
    groups, obs, members, lon_cells, lat_cells, lat_tiles = sizes
    chunks = lat_cells // LANES
    my_lon, my_lat = place[0], place[1]
    sources = (owners_in, order_in, lon_in, lat_in, offset_in, value_in, error_in)
    targets = (owners, order, lon, lat, offset, value, error)
    small = [
        pltpu.make_async_copy(source, target, small_sems.at[n])
        for n, (source, target) in enumerate(zip(sources, targets))
    ]
    for copy in small:
        copy.start()
    rows_t[...] = jnp.zeros_like(rows_t)
    for copy in small:
        copy.wait()

    def near(turn):
        tile_no = owners[order[turn]]
        lon_gap = tile_no // lat_tiles - my_lon
        lat_gap = tile_no % lat_tiles - my_lat
        return (jnp.abs(lon_gap) <= 1) & (jnp.abs(lat_gap) <= 1)

    touched = near(0)
    for turn in range(1, groups):
        touched = touched | near(turn)

    copies = [
        pltpu.make_async_copy(
            field.at[:, pl.ds(c * LANES, LANES)], tile.at[c], sems.at[c]
        )
        for c in range(chunks)
    ]

    @pl.when(touched)
    def _():
        for copy in copies:
            copy.start()

    lane = lax.broadcasted_iota(jnp.int32, (1, LANES), 1)
    values = jnp.zeros((1, LANES), jnp.float32)
    errors = jnp.zeros((1, LANES), jnp.float32)
    for turn in range(groups):
        group = order[turn]
        for k in range(obs):
            here = lane == turn * obs + k
            values = jnp.where(here, value[group, k], values)
            errors = jnp.where(here, error[group, k], errors)
    sub8 = lax.broadcasted_iota(jnp.int32, (8, LANES), 0)
    table[...] = jnp.where(sub8 == 0, values, errors)

    @pl.when(touched)
    def _():
        for copy in copies:
            copy.wait()

    @pl.loop(0, groups)
    def _(turn):
        @pl.when(near(turn))
        def _():
            group = order[turn]
            tile_no = owners[group]
            lon_base = (tile_no // lat_tiles - my_lon) * lon_cells
            lat_base = (tile_no % lat_tiles - my_lat) * lat_cells

            @pl.loop(0, obs)
            def _(k):
                p = lon_base + lon[group, k]
                q = lat_base + lat[group, k]
                a = offset[group, 0, k]
                b = offset[group, 1, k]
                inside = (p >= -1) & (p <= lon_cells) & (q >= -1) & (q <= lat_cells)

                @pl.when(inside)
                def _():
                    first = jnp.clip(q - 1, 0, lat_cells - 1) // LANES
                    last = jnp.clip(q + 1, 0, lat_cells - 1) // LANES

                    def part(chunk):
                        gap = (lane + chunk * LANES - q).astype(jnp.float32)
                        lat_hat = jnp.maximum(1.0 - jnp.abs(gap - b), 0.0)
                        total = jnp.zeros((members, LANES), jnp.float32)
                        for step in (-1, 0, 1):
                            row = p + step
                            hat = jnp.maximum(1.0 - jnp.abs(step - a), 0.0)
                            hat = jnp.where((row >= 0) & (row < lon_cells), hat, 0.0)
                            row = jnp.clip(row, 0, lon_cells - 1)
                            cells = tile[chunk, pl.ds(row, members, stride=lon_cells), :]
                            total = total + cells * (lat_hat * hat)
                        found = jnp.sum(total, axis=1, keepdims=True)
                        rows_t[...] += jnp.where(lane == turn * obs + k, found, 0.0)

                    part(first)

                    @pl.when(last != first)
                    def _():
                        part(last)


def split(x):
    high = x.astype(jnp.bfloat16)
    return high, (x - high.astype(jnp.float32)).astype(jnp.bfloat16)


def analysis_kernel(
    sizes, rows_t_ref, table, field, out, tile, done, reduced, factors, spreads, in_sems, out_sems
):
    groups, obs, members, lon_cells, lat_cells, lat_tiles = sizes
    count = groups * obs
    chunks = lat_cells // LANES
    reads = [
        pltpu.make_async_copy(field.at[:, pl.ds(c * LANES, LANES)], tile.at[c], in_sems.at[c])
        for c in range(chunks)
    ]
    writes = [
        pltpu.make_async_copy(done.at[c], out.at[:, pl.ds(c * LANES, LANES)], out_sems.at[c])
        for c in range(chunks)
    ]
    for copy in reads:
        copy.start()

    scale = float(members - 1)
    priors = rows_t_ref[...]
    mean = jnp.mean(priors, axis=0, keepdims=True)
    anomalies = priors - mean
    eye = (
        lax.broadcasted_iota(jnp.int32, (members, LANES), 0)
        == lax.broadcasted_iota(jnp.int32, (members, LANES), 1) % members
    ).astype(jnp.float32)
    both = lax.dot_general(
        anomalies,
        jnp.concatenate([anomalies, eye], axis=1),
        (((0,), (0,)), ((), ())),
        precision=HIGH,
        preferred_element_type=jnp.float32,
    )
    innovation = jnp.broadcast_to(table[0:1, :] - mean, (LANES, LANES)).T
    noise_row = table[1:2, :] * scale
    noise = jnp.broadcast_to(noise_row, (LANES, LANES)).T
    square = lax.broadcasted_iota(jnp.int32, (LANES, LANES), 0)
    across = lax.broadcasted_iota(jnp.int32, (LANES, LANES), 1)
    left_all = both[:, :LANES] + jnp.where(square == across, noise_row, 0.0)
    left_all = jnp.where(across == count, innovation, left_all)
    right_all = both[:, LANES:]

    sub = lax.broadcasted_iota(jnp.int32, (obs, LANES), 0)
    half = lax.broadcasted_iota(jnp.int32, (obs, LANES), 1) < members
    for g in range(groups):
        low = g * obs
        left = left_all[low : low + obs]
        right = right_all[low : low + obs]
        if g:
            change = lax.dot_general(
                factors[0:low, :],
                reduced[0:low, :],
                (((0,), (0,)), ((), ())),
                precision=HIGH,
                preferred_element_type=jnp.float32,
            )
            left = left - change[low : low + obs, :LANES]
            right = right - change[low : low + obs, LANES:]
        columns = [
            jnp.broadcast_to(left[:, low + i : low + i + 1], (obs, LANES)) for i in range(obs)
        ]
        inverses = jnp.zeros((obs, LANES), jnp.float32)
        shrinks = jnp.zeros((obs, LANES), jnp.float32)
        for j in range(obs):
            pivot = columns[j][j : j + 1, :]
            inverse = 1.0 / pivot
            shrink = 1.0 / (1.0 + jnp.sqrt(noise[low + j : low + j + 1, :] * inverse))
            inverses = jnp.where(sub == j, inverse, inverses)
            shrinks = jnp.where(sub == j, shrink, shrinks)
            if j == obs - 1:
                break
            factor = jnp.where(sub > j, columns[j] * inverse, 0.0)
            for i in range(j + 1, obs):
                columns[i] = columns[i] - factor * columns[i][j : j + 1, :]
            left = left - factor * left[j : j + 1, :]
            right = right - factor * (right[j : j + 1, :] * jnp.where(half[0:1], 1.0, shrink))
        innovations = jnp.broadcast_to(left[:, count : count + 1], (obs, LANES))
        spreads[low : low + obs, :] = inverses * (innovations - shrinks * right)
        factors[low : low + obs, :] = left * inverses
        reduced[low : low + obs, :LANES] = left
        reduced[low : low + obs, LANES:] = right * jnp.where(half, 1.0, shrinks)

    change = lax.dot_general(
        spreads[...],
        reduced[:, LANES:],
        (((0,), (0,)), ((), ())),
        precision=HIGH,
        preferred_element_type=jnp.float32,
    )[members : 2 * members, :members]
    high, low_part = split(change)
    weights = jnp.concatenate([high, high, low_part], axis=1)

    for c in range(chunks):
        reads[c].wait()

        @pl.loop(0, lon_cells // 4)
        def _(quad):
            cells = [
                tile[c, pl.ds(quad * 4 + r, members, stride=lon_cells), :] for r in range(4)
            ]
            block = jnp.concatenate(cells, axis=1)
            top, rest = split(block)
            new = block + jnp.dot(
                weights,
                jnp.concatenate([top, rest, top], axis=0),
                preferred_element_type=jnp.float32,
            )
            for r in range(4):
                done[c, pl.ds(quad * 4 + r, members, stride=lon_cells), :] = new[
                    :, r * LANES : (r + 1) * LANES
                ]

        writes[c].start()
    for copy in writes:
        copy.wait()


def shifted_sum(shard, axis, steps):
    size = lax.axis_size(axis)
    arrived = [
        lax.ppermute(shard, axis, [(i, (i + step) % size) for i in range(size)]) for step in steps
    ]
    for piece in arrived:
        shard = shard + piece
    return shard


def total_over_tiles(shard):
    shard = shifted_sum(shard, "lat", (1,))
    shard = shifted_sum(shard, "lon_0", (1, 2, 3))
    shard = shifted_sum(shard, "lon_2", (1, 2, 3))
    shard = shifted_sum(shard, "lon_1", (2, 4, 6))
    size = lax.axis_size("lon_1")
    return shard + lax.ppermute(shard, "lon_1", [(i, i ^ 1) for i in range(size)])


def body(ensemble, obs_lon, obs_lat, obs_offset, obs_value, obs_error, owners, group_order):
    members, lon_cells, lat_cells = ensemble.shape
    groups, obs = obs_lon.shape
    sizes = (groups, obs, members, lon_cells, lat_cells, lax.axis_size("lat"))
    chunks = lat_cells // LANES
    flat = ensemble.reshape(members * lon_cells, lat_cells)
    place = jnp.stack([lax.axis_index(LON), lax.axis_index("lat")]).astype(jnp.int32)
    smem = pl.BlockSpec(memory_space=pltpu.SMEM)
    vmem = pl.BlockSpec(memory_space=pltpu.VMEM)
    hbm = pl.BlockSpec(memory_space=pltpu.HBM)
    chunk_shape = (chunks, members * lon_cells, LANES)
    rows_t, table = pl.pallas_call(
        functools.partial(priors_kernel, sizes),
        out_shape=(
            jax.ShapeDtypeStruct((members, LANES), jnp.float32),
            jax.ShapeDtypeStruct((8, LANES), jnp.float32),
        ),
        in_specs=[smem] + [hbm] * 8,
        out_specs=(vmem, vmem),
        scratch_shapes=[
            pltpu.SMEM(obs_lon.shape, jnp.int32),
            pltpu.SMEM(obs_lat.shape, jnp.int32),
            pltpu.SMEM(obs_offset.shape, jnp.float32),
            pltpu.SMEM(obs_value.shape, jnp.float32),
            pltpu.SMEM(obs_error.shape, jnp.float32),
            pltpu.SMEM(owners.shape, jnp.int32),
            pltpu.SMEM(group_order.shape, jnp.int32),
            pltpu.VMEM(chunk_shape, jnp.float32),
            pltpu.SemaphoreType.DMA((7,)),
            pltpu.SemaphoreType.DMA((chunks,)),
        ],
        compiler_params=pltpu.CompilerParams(vmem_limit_bytes=16 << 20),
        name="priors",
    )(
        place,
        *(
            pltpu.with_memory_space_constraint(array, pltpu.HBM)
            for array in (
                obs_lon, obs_lat, obs_offset, obs_value, obs_error, owners, group_order, flat
            )
        ),
    )
    rows_t = total_over_tiles(rows_t)
    count = groups * obs
    result = pl.pallas_call(
        functools.partial(analysis_kernel, sizes),
        out_shape=jax.ShapeDtypeStruct(flat.shape, jnp.float32),
        in_specs=[vmem, vmem, hbm],
        out_specs=hbm,
        scratch_shapes=[
            pltpu.VMEM(chunk_shape, jnp.float32),
            pltpu.VMEM(chunk_shape, jnp.float32),
            pltpu.VMEM((count, 2 * LANES), jnp.float32),
            pltpu.VMEM((count, LANES), jnp.float32),
            pltpu.VMEM((count, LANES), jnp.float32),
            pltpu.SemaphoreType.DMA((chunks,)),
            pltpu.SemaphoreType.DMA((chunks,)),
        ],
        compiler_params=pltpu.CompilerParams(vmem_limit_bytes=32 << 20),
        name="analysis",
    )(rows_t, table, flat)
    return result.reshape(ensemble.shape)


def solution(mesh):
    torus = Mesh(
        mesh.devices.reshape(4, 8, 4, mesh.shape["lat"]), ("lon_0", "lon_1", "lon_2", "lat")
    )
    in_specs = (P(None, LON, "lat"), P(), P(), P(), P(), P(), P(), P())
    out_specs = P(None, LON, "lat")
    return jax.shard_map(body, mesh=torus, in_specs=in_specs, out_specs=out_specs, check_vma=False)
```

time: 764 us -> 54.7 us (0.07)
  the two profiles are of different devices: /device:TPU:1 before, /device:TPU:32 now
where the time goes in v1:
time: 54.7 us; the launch traced here: 54.4 us
  starting transfers between devices  21.4 us (39%)
  waiting for transfers between devices  17.9 us (33%)
  Pallas kernels  14.8 us (27%)
    ppermute x10, starting transfers between devices, shifted_sum(): lax.ppermute(shard, axis, [(i, (i + step) % size) for i in range(size)])  20.1 us
    ppermute x10, waiting for transfers between devices, shifted_sum(): lax.ppermute(shard, axis, [(i, (i + step) % size) for i in range(size)])  15 us
    pallas_call x1, Pallas kernels, body(): pl.pallas_call(functools.partial(analysis_kernel, sizes), out_shape=jax.S...  12.6 us
    ppermute x1, waiting for transfers between devices, total_over_tiles(): lax.ppermute(shard, 'lon_1', [(i, i ^ 1) for i in range(size)])  2.89 us
    pallas_call x1, Pallas kernels, body(): pl.pallas_call(functools.partial(priors_kernel, sizes), out_shape=(jax.Sh...  2.11 us
    ppermute x1, starting transfers between devices, total_over_tiles(): lax.ppermute(shard, 'lon_1', [(i, i ^ 1) for i in range(size)])  1.29 us
  transfers between devices with their start and end apart: 11, of which 8 were waited for; matrix products, arithmetic and copies ran while one was open for 0% of the time, Pallas kernels for 0%

profile of v1, /device:TPU:32, one launch (start us, length us, event | category | flops | bytes accessed | tf_op | source)
XLA Modules:
  0.0 54.4 jit_solution(17428484690690318971)
XLA Ops:
  0.0 0.1 pad_add_fusion.place
  0.1 2.1 %priors.1 = (f32[64,128]{1,0:T(8,128)S(1)}, f32[8,128]{1,0:T(8,128)S(1)}) custom-call(s32[2]{0:T(128)S(1)} %pad_add_fusion.place, s32[6,16]{1,0:T(8,128)} %lon_in.1, s32[6,16]{1,0:T(8,128)} %lat_in.1, f32[6,2,16]{2,1,0:T(2,128)} %offset_in.1, f32[6,16]{1,0:T(8,128)} %value_in.1, f32[6,16]{1,0:T(8,128)} %error_in.1, s32[6]{0:T(128)} %owners_in.1, s32[6]{0:T(128)} %order_in.1, ...), custom_call_target="tpu_custom_call" | custom-call | tf_op jit(solution)/shard_map/priors/pallas_call | solution.py:268
  2.2 0.1 collective-permute-start
  2.3 1.2 %collective-permute-done = f32[64,128]{1,0:T(8,128)S(1)} collective-permute-done((f32[64,128]{1,0:T(8,128)S(1)}, f32[64,128]{1,0:T(8,128)S(1)}, u32[]{:S(2)}, u32[]{:S(2)}) %collective-permute-start) | collective-permute-done | bytes 32800 | tf_op jit(solution)/shard_map/ppermute | solution.py:241
  3.5 2.8 %collective-permute-start.3 = (f32[64,128]{1,0:T(8,128)S(1)}, f32[64,128]{1,0:T(8,128)S(1)}, u32[]{:S(2)}, u32[]{:S(2)}) collective-permute-start(f32[64,128]{1,0:T(8,128)S(1)} %add.41), channel_id=1, source_target_pairs={{0,192},{64,0},{128,64},{192,128},{1,193},{65,1},{129,65},{193,129... | collective-permute-start | bytes 98312 | tf_op jit(solution)/shard_map/ppermute | solution.py:241
  6.3 0.8 %collective-permute-start.2 = (f32[64,128]{1,0:T(8,128)S(1)}, f32[64,128]{1,0:T(8,128)S(1)}, u32[]{:S(2)}, u32[]{:S(2)}) collective-permute-start(f32[64,128]{1,0:T(8,128)S(1)} %add.41), channel_id=1, source_target_pairs={{0,128},{64,192},{128,0},{192,64},{1,129},{65,193},{129,1},{193,65... | collective-permute-start | bytes 98312 | tf_op jit(solution)/shard_map/ppermute | solution.py:241
  7.1 0.9 %collective-permute-start.1 = (f32[64,128]{1,0:T(8,128)S(1)}, f32[64,128]{1,0:T(8,128)S(1)}, u32[]{:S(2)}, u32[]{:S(2)}) collective-permute-start(f32[64,128]{1,0:T(8,128)S(1)} %add.41), channel_id=1, source_target_pairs={{0,64},{64,128},{128,192},{192,0},{1,65},{65,129},{129,193},{193,1... | collective-permute-start | bytes 98312 | tf_op jit(solution)/shard_map/ppermute | solution.py:241
  7.9 0.1 collective-permute-done.3
  8.1 3.6 %collective-permute-done.2 = f32[64,128]{1,0:T(8,128)S(1)} collective-permute-done((f32[64,128]{1,0:T(8,128)S(1)}, f32[64,128]{1,0:T(8,128)S(1)}, u32[]{:S(2)}, u32[]{:S(2)}) %collective-permute-start.2) | collective-permute-done | bytes 32800 | tf_op jit(solution)/shard_map/ppermute | solution.py:241
  11.7 0.5 collective-permute-done.1
  12.2 3.1 %collective-permute-start.6 = (f32[64,128]{1,0:T(8,128)S(1)}, f32[64,128]{1,0:T(8,128)S(1)}, u32[]{:S(2)}, u32[]{:S(2)}) collective-permute-start(f32[64,128]{1,0:T(8,128)S(1)} %add_add_fusion.2), channel_id=1, source_target_pairs={{0,6},{2,0},{4,2},{6,4},{1,7},{3,1},{5,3},{7,5},{8,14},{10,8},{12,... | collective-permute-start | bytes 98312 | tf_op jit(solution)/shard_map/ppermute | solution.py:241
  15.3 0.6 %collective-permute-start.5 = (f32[64,128]{1,0:T(8,128)S(1)}, f32[64,128]{1,0:T(8,128)S(1)}, u32[]{:S(2)}, u32[]{:S(2)}) collective-permute-start(f32[64,128]{1,0:T(8,128)S(1)} %add_add_fusion.2), channel_id=1, source_target_pairs={{0,4},{2,6},{4,0},{6,2},{1,5},{3,7},{5,1},{7,3},{8,12},{10,14},{12... | collective-permute-start | bytes 98312 | tf_op jit(solution)/shard_map/ppermute | solution.py:241
  15.9 1.0 %collective-permute-start.4 = (f32[64,128]{1,0:T(8,128)S(1)}, f32[64,128]{1,0:T(8,128)S(1)}, u32[]{:S(2)}, u32[]{:S(2)}) collective-permute-start(f32[64,128]{1,0:T(8,128)S(1)} %add_add_fusion.2), channel_id=1, source_target_pairs={{0,2},{2,4},{4,6},{6,0},{1,3},{3,5},{5,7},{7,1},{8,10},{10,12},{12... | collective-permute-start | bytes 98312 | tf_op jit(solution)/shard_map/ppermute | solution.py:241
  16.9 0.0 collective-permute-done.6
  16.9 3.8 %collective-permute-done.5 = f32[64,128]{1,0:T(8,128)S(1)} collective-permute-done((f32[64,128]{1,0:T(8,128)S(1)}, f32[64,128]{1,0:T(8,128)S(1)}, u32[]{:S(2)}, u32[]{:S(2)}) %collective-permute-start.5) | collective-permute-done | bytes 32800 | tf_op jit(solution)/shard_map/ppermute | solution.py:241
  20.7 0.4 collective-permute-done.4
  21.1 8.4 %collective-permute-start.9 = (f32[64,128]{1,0:T(8,128)S(1)}, f32[64,128]{1,0:T(8,128)S(1)}, u32[]{:S(2)}, u32[]{:S(2)}) collective-permute-start(f32[64,128]{1,0:T(8,128)S(1)} %add_add_fusion.1), channel_id=1, source_target_pairs={{0,48},{8,56},{16,0},{24,8},{32,16},{40,24},{48,32},{56,40},{1,49}... | collective-permute-start | bytes 98312 | tf_op jit(solution)/shard_map/ppermute | solution.py:241
  29.5 0.7 %collective-permute-start.8 = (f32[64,128]{1,0:T(8,128)S(1)}, f32[64,128]{1,0:T(8,128)S(1)}, u32[]{:S(2)}, u32[]{:S(2)}) collective-permute-start(f32[64,128]{1,0:T(8,128)S(1)} %add_add_fusion.1), channel_id=1, source_target_pairs={{0,32},{8,40},{16,48},{24,56},{32,0},{40,8},{48,16},{56,24},{1,33}... | collective-permute-start | bytes 98312 | tf_op jit(solution)/shard_map/ppermute | solution.py:241
  30.2 1.8 %collective-permute-start.7 = (f32[64,128]{1,0:T(8,128)S(1)}, f32[64,128]{1,0:T(8,128)S(1)}, u32[]{:S(2)}, u32[]{:S(2)}) collective-permute-start(f32[64,128]{1,0:T(8,128)S(1)} %add_add_fusion.1), channel_id=1, source_target_pairs={{0,16},{8,24},{16,32},{24,40},{32,48},{40,56},{48,0},{56,8},{1,17}... | collective-permute-start | bytes 98312 | tf_op jit(solution)/shard_map/ppermute | solution.py:241
  32.0 5.4 %collective-permute-done.8 = f32[64,128]{1,0:T(8,128)S(1)} collective-permute-done((f32[64,128]{1,0:T(8,128)S(1)}, f32[64,128]{1,0:T(8,128)S(1)}, u32[]{:S(2)}, u32[]{:S(2)}) %collective-permute-start.8) | collective-permute-done | bytes 32800 | tf_op jit(solution)/shard_map/ppermute | solution.py:241
  37.3 0.0 collective-permute-done.7
  37.4 1.3 %collective-permute-start.10 = (f32[64,128]{1,0:T(8,128)S(1)}, f32[64,128]{1,0:T(8,128)S(1)}, u32[]{:S(2)}, u32[]{:S(2)}) collective-permute-start(f32[64,128]{1,0:T(8,128)S(1)} %add_add_fusion), channel_id=1, source_target_pairs={{0,8},{8,0},{16,24},{24,16},{32,40},{40,32},{48,56},{56,48},{1,9},... | collective-permute-start | bytes 98312 | tf_op jit(solution)/shard_map/ppermute | solution.py:254
  38.7 2.9 %collective-permute-done.10 = f32[64,128]{1,0:T(8,128)S(1)} collective-permute-done((f32[64,128]{1,0:T(8,128)S(1)}, f32[64,128]{1,0:T(8,128)S(1)}, u32[]{:S(2)}, u32[]{:S(2)}) %collective-permute-start.10) | collective-permute-done | bytes 32800 | tf_op jit(solution)/shard_map/ppermute | solution.py:254
  41.6 12.6 %analysis.1 = f32[1024,1024]{1,0:T(8,128)} custom-call(f32[64,128]{1,0:T(8,128)S(1)} %add.51.rows_t_ref, f32[8,128]{1,0:T(8,128)S(1)} %get-tuple-element.8.table, f32[1024,1024]{1,0:T(8,128)S(1)} %bitcast.5), custom_call_target="tpu_custom_call" | custom-call | tf_op jit(solution)/shard_map/analysis/pallas_call | solution.py:301
  (8 shorter events, 0.0 us)
Async XLA Ops:
  0.0 41.6 %copy-start = (f32[64,16,1024]{2,1,0:T(8,128)S(1)}, f32[64,16,1024]{2,1,0:T(8,128)}, u32[]{:S(2)}) copy-start(f32[64,16,1024]{2,1,0:T(8,128)} %param.8) | copy-start | bytes 12582916
  2.2 1.3 %collective-permute-start = (f32[64,128]{1,0:T(8,128)S(1)}, f32[64,128]{1,0:T(8,128)S(1)}, u32[]{:S(2)}, u32[]{:S(2)}) collective-permute-start(f32[64,128]{1,0:T(8,128)S(1)} %get-tuple-element.7), channel_id=1, source_target_pairs={{0,1},{1,0},{2,3},{3,2},{4,5},{5,4},{6,7},{7,6},{8,9},{9,8},{10,11... | collective-permute-start | bytes 98312 | tf_op jit(solution)/shard_map/ppermute | solution.py:241
  3.5 4.6 %collective-permute-start.3 = (f32[64,128]{1,0:T(8,128)S(1)}, f32[64,128]{1,0:T(8,128)S(1)}, u32[]{:S(2)}, u32[]{:S(2)}) collective-permute-start(f32[64,128]{1,0:T(8,128)S(1)} %add.41), channel_id=1, source_target_pairs={{0,192},{64,0},{128,64},{192,128},{1,193},{65,1},{129,65},{193,129... | collective-permute-start | bytes 98312 | tf_op jit(solution)/shard_map/ppermute | solution.py:241
  6.3 5.4 %collective-permute-start.2 = (f32[64,128]{1,0:T(8,128)S(1)}, f32[64,128]{1,0:T(8,128)S(1)}, u32[]{:S(2)}, u32[]{:S(2)}) collective-permute-start(f32[64,128]{1,0:T(8,128)S(1)} %add.41), channel_id=1, source_target_pairs={{0,128},{64,192},{128,0},{192,64},{1,129},{65,193},{129,1},{193,65... | collective-permute-start | bytes 98312 | tf_op jit(solution)/shard_map/ppermute | solution.py:241
  7.1 5.1 %collective-permute-start.1 = (f32[64,128]{1,0:T(8,128)S(1)}, f32[64,128]{1,0:T(8,128)S(1)}, u32[]{:S(2)}, u32[]{:S(2)}) collective-permute-start(f32[64,128]{1,0:T(8,128)S(1)} %add.41), channel_id=1, source_target_pairs={{0,64},{64,128},{128,192},{192,0},{1,65},{65,129},{129,193},{193,1... | collective-permute-start | bytes 98312 | tf_op jit(solution)/shard_map/ppermute | solution.py:241
  12.2 4.7 %collective-permute-start.6 = (f32[64,128]{1,0:T(8,128)S(1)}, f32[64,128]{1,0:T(8,128)S(1)}, u32[]{:S(2)}, u32[]{:S(2)}) collective-permute-start(f32[64,128]{1,0:T(8,128)S(1)} %add_add_fusion.2), channel_id=1, source_target_pairs={{0,6},{2,0},{4,2},{6,4},{1,7},{3,1},{5,3},{7,5},{8,14},{10,8},{12,... | collective-permute-start | bytes 98312 | tf_op jit(solution)/shard_map/ppermute | solution.py:241
  15.3 5.4 %collective-permute-start.5 = (f32[64,128]{1,0:T(8,128)S(1)}, f32[64,128]{1,0:T(8,128)S(1)}, u32[]{:S(2)}, u32[]{:S(2)}) collective-permute-start(f32[64,128]{1,0:T(8,128)S(1)} %add_add_fusion.2), channel_id=1, source_target_pairs={{0,4},{2,6},{4,0},{6,2},{1,5},{3,7},{5,1},{7,3},{8,12},{10,14},{12... | collective-permute-start | bytes 98312 | tf_op jit(solution)/shard_map/ppermute | solution.py:241
  15.9 5.1 %collective-permute-start.4 = (f32[64,128]{1,0:T(8,128)S(1)}, f32[64,128]{1,0:T(8,128)S(1)}, u32[]{:S(2)}, u32[]{:S(2)}) collective-permute-start(f32[64,128]{1,0:T(8,128)S(1)} %add_add_fusion.2), channel_id=1, source_target_pairs={{0,2},{2,4},{4,6},{6,0},{1,3},{3,5},{5,7},{7,1},{8,10},{10,12},{12... | collective-permute-start | bytes 98312 | tf_op jit(solution)/shard_map/ppermute | solution.py:241
  21.1 10.9 %collective-permute-start.9 = (f32[64,128]{1,0:T(8,128)S(1)}, f32[64,128]{1,0:T(8,128)S(1)}, u32[]{:S(2)}, u32[]{:S(2)}) collective-permute-start(f32[64,128]{1,0:T(8,128)S(1)} %add_add_fusion.1), channel_id=1, source_target_pairs={{0,48},{8,56},{16,0},{24,8},{32,16},{40,24},{48,32},{56,40},{1,49}... | collective-permute-start | bytes 98312 | tf_op jit(solution)/shard_map/ppermute | solution.py:241
  29.5 7.8 %collective-permute-start.8 = (f32[64,128]{1,0:T(8,128)S(1)}, f32[64,128]{1,0:T(8,128)S(1)}, u32[]{:S(2)}, u32[]{:S(2)}) collective-permute-start(f32[64,128]{1,0:T(8,128)S(1)} %add_add_fusion.1), channel_id=1, source_target_pairs={{0,32},{8,40},{16,48},{24,56},{32,0},{40,8},{48,16},{56,24},{1,33}... | collective-permute-start | bytes 98312 | tf_op jit(solution)/shard_map/ppermute | solution.py:241
  30.2 7.2 %collective-permute-start.7 = (f32[64,128]{1,0:T(8,128)S(1)}, f32[64,128]{1,0:T(8,128)S(1)}, u32[]{:S(2)}, u32[]{:S(2)}) collective-permute-start(f32[64,128]{1,0:T(8,128)S(1)} %add_add_fusion.1), channel_id=1, source_target_pairs={{0,16},{8,24},{16,32},{24,40},{32,48},{40,56},{48,0},{56,8},{1,17}... | collective-permute-start | bytes 98312 | tf_op jit(solution)/shard_map/ppermute | solution.py:241
  37.4 4.2 %collective-permute-start.10 = (f32[64,128]{1,0:T(8,128)S(1)}, f32[64,128]{1,0:T(8,128)S(1)}, u32[]{:S(2)}, u32[]{:S(2)}) collective-permute-start(f32[64,128]{1,0:T(8,128)S(1)} %add_add_fusion), channel_id=1, source_target_pairs={{0,8},{8,0},{16,24},{24,16},{32,40},{40,32},{48,56},{56,48},{1,9},... | collective-permute-start | bytes 98312 | tf_op jit(solution)/shard_map/ppermute | solution.py:254
